TPU v7x, 32 devices: a whole 2x2x4 slice. The times are simulated.
32 devices in a mesh: row: 16 (over z, y, core), col: 2 (over x).
Axes of the slice: x: 2, y: 2, z: 4, core: 2. Of those that a mesh axis runs over, the one named last changes fastest.
Arguments:
- jacobian: bfloat16 [512, 256, 128], P(('col', 'row')), may hold values from -1.5 to 1.5
- weights: bfloat16 [32, 512, 256], P('row', 'col'), may hold values from 0.25 to 4
- panel_weights: bfloat16 [512, 256], P(('col', 'row')), may hold values from 0.25 to 4
- damping: float32 [32, 128], P('row'), may hold values from 0.01 to 1
- panel_inverse: float32 [128, 128], replicated, may hold values from -0.12 to 0.12
Outputs:
- schur: float32 [4096, 65536], P('row', 'col')
All inputs are finite; a program needn't handle non-finite values.
Results may differ from a plain program's by a relative error of at most 0.0022.
Values may be sent and summed in bfloat16 or wider, within the bound.
No kernel may reach another device: no remote copies, remote signals or barrier semaphores. Data moves between devices by JAX's collectives and lax.ppermute only.
A program may use at most 128 MiB of HBM per device.

v0:
```python
import jax
import jax.numpy as jnp
from jax import lax
from jax.sharding import PartitionSpec as P

HIGHEST = lax.Precision.HIGHEST


def broadcast(value, axis, root):
    mine = lax.axis_index(axis) == root
    return lax.psum(jnp.where(mine, value, jnp.zeros_like(value)), axis)


def shards(jacobian, weights, panel_weights, damping, panel_inverse):
    per_dev, sample_rows, param_width = jacobian.shape
    slab_rows, col_block, _ = weights.shape
    row_count = lax.axis_size("row")
    col_count = lax.axis_size("col")
    row_index = lax.axis_index("row")
    col_index = lax.axis_index("col")
    station_total = col_block * col_count
    panel_id = station_total - 1
    slab_ids = row_index * slab_rows + jnp.arange(slab_rows, dtype=jnp.int32)
    col_base = col_index * col_block
    col_ids = col_base + jnp.arange(col_block, dtype=jnp.int32)
    station_piece = lax.all_gather(jacobian, "row", axis=0, tiled=True)
    how_many = station_piece.shape[0]
    piece_ids = col_base + jnp.arange(how_many, dtype=jnp.int32)
    self_pair = slab_ids[:, None] == piece_ids[None, :]
    scaled = weights.astype(jnp.float32)[..., None] * station_piece.astype(jnp.float32)[None]
    scaled = jnp.where(self_pair[:, :, None, None], 0.0, scaled).astype(jnp.bfloat16)
    gram_part = jnp.einsum(
        "ijra,jrb->iab", scaled, station_piece, preferred_element_type=jnp.float32
    )
    gathered = station_piece
    scaled_all = scaled
    gram_part, gathered, scaled_all = (gram_part, gathered, scaled_all)
    home_col = row_index * slab_rows // col_block
    offset = row_index * slab_rows % col_block
    my_slab = lax.dynamic_slice_in_dim(gathered, offset, slab_rows, 0)
    slab_jac = broadcast(my_slab, "col", home_col)
    coupling = jnp.einsum(
        "ijra,irb->iajb", scaled_all, slab_jac, preferred_element_type=jnp.float32
    )
    gram_sum = lax.psum(gram_part, "col")
    identity = jnp.eye(param_width, dtype=jnp.float32)
    diag_block = (
        gram_sum + identity[None] * (jnp.diagonal(gram_sum, axis1=1, axis2=2) * damping)[:, None, :]
    )
    on_self = slab_ids[:, None] == col_ids[None, :]
    hessian = jnp.where(on_self[:, None, :, None], diag_block[:, :, None, :], coupling)
    local_factor = jnp.einsum(
        "iac,cb->iab",
        hessian[:, :, col_block - 1, :],
        panel_inverse,
        precision=HIGHEST,
        preferred_element_type=jnp.float32,
    )
    panel_factor, panel_jac = (
        broadcast(local_factor.astype(jnp.bfloat16), "col", col_count - 1).astype(
            local_factor.dtype
        ),
        broadcast(gathered[col_block - 1], "col", col_count - 1),
    )
    own_ids = (col_index * row_count + row_index) * per_dev + jnp.arange(per_dev, dtype=jnp.int32)
    scaled_rows = panel_weights.astype(jnp.float32)[..., None] * jacobian.astype(jnp.float32)
    scaled_rows = jnp.where((own_ids == panel_id)[:, None, None], 0.0, scaled_rows).astype(
        jnp.bfloat16
    )
    row_part = jnp.einsum("jra,rb->jab", scaled_rows, panel_jac, preferred_element_type=jnp.float32)
    station_piece = lax.all_gather(row_part.astype(jnp.bfloat16), "row", axis=0, tiled=True).astype(
        jnp.float32
    )
    how_many = station_piece.shape[0]
    current = lax.slice_in_dim(hessian, 0, how_many, axis=2)
    correction = jnp.einsum(
        "iac,jcb->iajb",
        panel_factor,
        station_piece,
        precision=HIGHEST,
        preferred_element_type=jnp.float32,
    )
    piece_ids = col_base + jnp.arange(how_many, dtype=jnp.int32)
    result = jnp.where(
        (piece_ids == panel_id)[None, None, :, None],
        panel_factor[:, :, None, :],
        current - correction,
    )
    return result.reshape(slab_rows * param_width, how_many * param_width)


def solution(mesh):
    return jax.shard_map(
        shards,
        mesh=mesh,
        in_specs=(
            P(("col", "row"), None, None),
            P("row", "col", None),
            P(("col", "row"), None),
            P("row", None),
            P(),
        ),
        out_specs=P("row", "col"),
        check_vma=False,
    )
```

profile of v0, /device:TPU:0, one launch (start us, length us, event | category | flops | bytes accessed | tf_op | source)
XLA Modules:
  0.0 486.4 jit_solution(10741653485367392175)
XLA Ops:
  6.5 0.7 all-gather.3.cloned.1.call-update
  7.3 1.0 convert_element_type.35
  8.5 130.7 %all-gather.3.cloned.1.call-done = bf16[256,256,128]{2,1,0:T(8,128)(2,1)} async-done(((bf16[16,256,128]{2,1,0:T(8,128)(2,1)}), bf16[256,256,128]{2,1,0:T(8,128)(2,1)}) %all-gather.3.cloned.1.call-update) | async-done | bytes 16777232 | tf_op jit(solution)/shard_map/all_gather | solution.py:26
  139.1 0.9 constant_dynamic-slice_fusion
  140.2 9.4 %convert_element_type.36 = f32[256,256,128]{2,1,0:T(8,128)S(1)} convert(bf16[256,256,128]{2,1,0:T(8,128)(2,1)} %all-gather.3.cloned.1.call-done) | non-fusion elementwise | flops 8388608 | bytes 50331648 | tf_op jit(solution)/shard_map/convert_element_type | solution.py:30
  149.6 11.7 %copy-done.1 = f32[256,256,128]{2,1,0:T(8,128)} copy-done((f32[256,256,128]{2,1,0:T(8,128)}, f32[256,256,128]{2,1,0:T(8,128)S(1)}, u32[]{:S(2)}) %copy-start.1) | copy-done | bytes 33554456
  161.3 47.9 %fusion.12 = f32[2,128,128]{2,1,0:T(8,128)} fusion(bf16[256,256,128]{2,1,0:T(8,128)(2,1)} %all-gather.3.cloned.1.call-done, f32[256,256,128]{2,1,0:T(8,128)S(1)} %convert_element_type.36, f32[2,256,256]{2,1,0:T(8,128)S(1)} %convert_element_type.35, pred[2,256]{1,0:T(4,128)(4,1)S(1)} %broadcast_compare_fusion), kind=kOutput, calls=%fused_computation.19 | convolution fusion | flops 4345298944 | bytes 50987520 | tf_op jit(solution)/shard_map/ijra,jrb->iab/dot_general | solution.py:32
  209.2 0.7 broadcast_select_fusion
  210.0 1.5 fusion.20
  211.5 17.5 %all-reduce.5.cloned.1.call-done = f32[2,128,128]{2,1,0:T(8,128)} async-done(((f32[2,128,128]{2,1,0:T(8,128)}), f32[2,128,128]{2,1,0:T(8,128)}) %all-reduce.5.cloned.1.call-update) | async-done | bytes 131088 | tf_op jit(solution)/shard_map/psum | solution.py:45
  228.9 5.5 %copy.37 = f32[2,128,128]{0,2,1:T(8,128)} copy(f32[2,128,128]{2,1,0:T(8,128)} %all-reduce.5.cloned.1.call-done) | data formatting | bytes 262144 | tf_op jit(solution)/shard_map/psum | solution.py:45
  234.4 1.8 gather_fusion
  236.3 0.9 multiply_add_fusion
  237.4 15.3 %all-reduce.7.cloned.1.call-done = bf16[2,256,128]{1,2,0:T(8,128)(2,1)} async-done(((bf16[2,256,128]{1,2,0:T(8,128)(2,1)}), bf16[2,256,128]{1,2,0:T(8,128)(2,1)}) %all-reduce.7.cloned.1.call-update) | async-done | bytes 131088 | tf_op jit(solution)/shard_map/psum | solution.py:11
  252.7 23.6 %bitcast_select_fusion = f32[2,128,256,128]{1,3,2,0:T(8,128)S(1)} fusion(f32[2,128,128]{1,2,0:T(8,128)S(1)} %copy.39, pred[2,256]{1,0:T(4,128)(4,1)S(1)} %broadcast_compare_fusion, f32[256,256,128]{2,1,0:T(8,128)} %copy-done.1, f32[2,256,256]{2,1,0:T(8,128)S(1)} %convert_element_type.35, bf16[2,256,128]{1,2,0:T(8,128)(2,1)} %all-reduce.7.cloned.1.call-done), kind=kOutput, calls=%fused_computation.5 | convolution fusion | flops 4353687552 | bytes 67895808 | tf_op jit(solution)/shard_map/ijra,irb->iajb/dot_general | solution.py:42
  276.3 11.7 %copy-done.2 = f32[2,128,256,128]{1,3,2,0:T(8,128)} copy-done((f32[2,128,256,128]{1,3,2,0:T(8,128)}, f32[2,128,256,128]{1,3,2,0:T(8,128)S(1)}, u32[]{:S(2)}) %copy-start.2) | copy-done | bytes 33554456
  288.0 1.0 fusion.15
  289.3 21.5 %all-reduce.9.cloned.1.call-done = (bf16[2,128,128]{2,1,0:T(8,128)(2,1)}, bf16[256,128]{1,0:T(8,128)(2,1)}) async-done(((bf16[2,128,128]{2,1,0:T(8,128)(2,1)}, bf16[256,128]{1,0:T(8,128)(2,1)}), (bf16[2,128,128]{2,1,0:T(8,128)(2,1)}, bf16[256,128]{1,0:T(8,128)(2,1)})) %all-reduce.9.cloned.1.call-update) | async-done | bytes 131088 | tf_op jit(solution)/shard_map/psum | solution.py:11
  310.8 2.9 convolution_convert_fusion
  313.7 0.9 copy.42
  314.7 74.1 %all-gather.5.cloned.1.call-done = bf16[256,128,128]{2,1,0:T(8,128)(2,1)} async-done(((bf16[16,128,128]{2,1,0:T(8,128)(2,1)}), bf16[256,128,128]{2,1,0:T(8,128)(2,1)}) %all-gather.5.cloned.1.call-update) | async-done | bytes 8388624 | tf_op jit(solution)/shard_map/all_gather | solution.py:71
  388.8 28.2 %subtract_select_fusion = f32[2,128,256,128]{1,3,2,0:T(8,128)} fusion(f32[2,128,256,128]{1,3,2,0:T(8,128)} %copy-done.2, f32[2,128,128]{1,2,0:T(8,128)S(1)} %copy.42, pred[256]{0:T(512)(128)(4,1)S(1)} %broadcast_compare_fusion.1, bf16[256,128,128]{2,1,0:T(8,128)(2,1)} %all-gather.5.cloned.1.call-done, bf16[2,128,128]{2,1,0:T(8,128)(2,1)} %get-tuple-element.5), kind=kOutput, calls=%fused_computation.6 | convolution fusion | flops 2164260864 | bytes 75694336 | tf_op jit(solution)/shard_map/iac,jcb->iajb/dot_general | solution.py:76
  417.0 31.1 %copy.45 = f32[2,128,256,128]{3,2,1,0:T(8,128)} copy(f32[2,128,256,128]{1,3,2,0:T(8,128)} %subtract_select_fusion) | data formatting | bytes 67108864 | tf_op jit(solution)/shard_map/jit(_where)/select_n | solution.py:84
  448.1 31.8 %copy.56 = f32[32,8,256,128]{3,1,2,0:T(8,128)} copy(f32[32,8,256,128]{3,2,1,0:T(8,128)} %bitcast.47) | data formatting | bytes 67108864
  (31 shorter events, 0.8 us)
Async XLA Ops:
  6.5 281.5 %copy-start = (f32[128,128]{1,0:T(8,128)S(1)}, f32[128,128]{1,0:T(8,128)}, u32[]{:S(2)}) copy-start(f32[128,128]{1,0:T(8,128)} %param.9) | copy-start | bytes 196612
  6.5 132.6 %all-gather.3.cloned.1.call-start = ((), (), s32[]{:S(2)}) async-start(), calls=%async_computation | async-start | bytes 17825792 | tf_op jit(solution)/shard_map/all_gather | solution.py:26
  7.3 221.7 %all-reduce.5.cloned.1.call-start = ((), (), s32[]{:S(2)}) async-start(), calls=%async_computation.1 | async-start | bytes 262144 | tf_op jit(solution)/shard_map/psum | solution.py:45
  149.6 11.7 %copy-start.1 = (f32[256,256,128]{2,1,0:T(8,128)}, f32[256,256,128]{2,1,0:T(8,128)S(1)}, u32[]{:S(2)}) copy-start(f32[256,256,128]{2,1,0:T(8,128)S(1)} %convert_element_type.36) | copy-start | bytes 100663296
  161.3 75.0 %copy-start.5 = (f32[2,128]{1,0:T(2,128)S(1)}, f32[2,128]{1,0:T(2,128)}, u32[]{:S(2)}) copy-start(f32[2,128]{1,0:T(2,128)} %param.8) | copy-start | bytes 3076
  209.2 43.5 %all-reduce.7.cloned.1.call-start = ((), (), s32[]{:S(2)}) async-start(), calls=%async_computation.2 | async-start | bytes 262144 | tf_op jit(solution)/shard_map/psum | solution.py:11
  209.9 100.9 %all-reduce.9.cloned.1.call-start = ((), (), s32[]{:S(2)}) async-start(), calls=%async_computation.4 | async-start | bytes 262144 | tf_op jit(solution)/shard_map/psum | solution.py:11
  237.3 52.0 %copy-start.4 = (bf16[16,256]{1,0:T(8,128)(2,1)S(1)}, bf16[16,256]{1,0:T(8,128)(2,1)}, u32[]{:S(2)}) copy-start(bf16[16,256]{1,0:T(8,128)(2,1)} %param.7) | copy-start | bytes 24580
  237.3 73.5 %copy-start.3 = (bf16[16,256,128]{2,1,0:T(8,128)(2,1)S(1)}, bf16[16,256,128]{2,1,0:T(8,128)(2,1)}, u32[]{:S(2)}) copy-start(bf16[16,256,128]{2,1,0:T(8,128)(2,1)} %param.5) | copy-start | bytes 3145732
  276.3 11.7 %copy-start.2 = (f32[2,128,256,128]{1,3,2,0:T(8,128)}, f32[2,128,256,128]{1,3,2,0:T(8,128)S(1)}, u32[]{:S(2)}) copy-start(f32[2,128,256,128]{1,3,2,0:T(8,128)S(1)} %bitcast_select_fusion) | copy-start | bytes 100663296
  289.1 99.7 %all-gather.5.cloned.1.call-start = ((), (), s32[]{:S(2)}) async-start(), calls=%async_computation.3 | async-start | bytes 8912896 | tf_op jit(solution)/shard_map/all_gather | solution.py:71
Sparse Core Ops, SparseCore 0:
  9.5 129.5 all-gather.2
  209.3 19.5 all-reduce.4
  231.2 21.4 all-reduce.6
  289.2 21.5 all-reduce.8
  313.8 74.8 all-gather.4
where the time goes:
time: 488 us; the launch traced here: 486 us
  waiting for transfers between devices  260 us (53%)
  matrix products  104 us (21%)
  local copies, waits for them, and re-layouts  95.7 us (20%)
  other arithmetic  13.6 us (3%)
  between operations  13.3 us (3%)
    all_gather x1, waiting for transfers between devices, shards(): station_piece = lax.all_gather(jacobian, 'row', axis=0, tiled=True)  131 us
    all_gather x1, waiting for transfers between devices, shards(): lax.all_gather(row_part.astype(jnp.bfloat16), 'row', axis=0, tiled=True)  74.1 us
    unnamed x14, local copies, waits for them, and re-layouts  55.3 us
    dot_general x1, matrix products, shards(): jnp.einsum('ijra,jrb->iab', scaled, station_piece, preferred_element_type...  47.9 us
    psum x2, waiting for transfers between devices, broadcast(): return lax.psum(jnp.where(mine, value, jnp.zeros_like(value)), axis)  36.8 us
    select_n x1, local copies, waits for them, and re-layouts, shards(): jnp.where((piece_ids == panel_id)[None, None, :, None], panel_factor[:, :...  31.1 us
    dot_general x1, matrix products, shards(): jnp.einsum('iac,jcb->iajb', panel_factor, station_piece, precision=HIGHES...  28.2 us
    dot_general x1, matrix products, shards(): jnp.einsum('ijra,irb->iajb', scaled_all, slab_jac, preferred_element_type...  23.6 us
  transfers between devices with their start and end apart: 5, of which 5 were waited for; matrix products, arithmetic and copies ran while one was open for 3% of the time, Pallas kernels for 0%

commit v1 on v0

--- a/solution.py
+++ b/solution.py
@@ -42,7 +42,7 @@
     coupling = jnp.einsum(
         "ijra,irb->iajb", scaled_all, slab_jac, preferred_element_type=jnp.float32
     )
-    gram_sum = lax.psum(gram_part, "col")
+    gram_sum = jnp.sum(lax.all_gather(gram_part, "col"), axis=0)
     identity = jnp.eye(param_width, dtype=jnp.float32)
     diag_block = (
         gram_sum + identity[None] * (jnp.diagonal(gram_sum, axis1=1, axis2=2) * damping)[:, None, :]

time: 488 us -> 445 us (0.912)
  waiting for transfers between devices: 260 us -> 225 us
  local copies, waits for them, and re-layouts: 95.7 us -> 83.2 us
  blocking collectives: 0 us -> 6.33 us
    psum x1 -> x0, waiting for transfers between devices: 17.5 us -> none  [shards(): gram_sum = lax.psum(gram_part, 'col')]
    psum x2, waiting for transfers between devices: 36.8 us -> 19.6 us  [broadcast(): return lax.psum(jnp.where(mine, value, jnp.zeros_like(value)), axis)]
    unnamed x14, local copies, waits for them, and re-layouts: 55.3 us -> 43.6 us
    all_gather x0 -> x1, blocking collectives: none -> 6.33 us  [shards(): gram_sum = jnp.sum(lax.all_gather(gram_part, 'col'), axis=0)]
    psum x1 -> x0, local copies, waits for them, and re-layouts: 5.49 us -> none  [shards(): gram_sum = lax.psum(gram_part, 'col')]
  transfers between devices with their start and end apart: 5 -> 4, of which waited for: 5 -> 3; matrix products, arithmetic and copies ran while one was open for 3% -> 15% of each run, Pallas kernels for 0% -> 0%
where the time goes in v1:
time: 445 us; the launch traced here: 444 us
  waiting for transfers between devices  225 us (51%)
  matrix products  103 us (23%)
  local copies, waits for them, and re-layouts  83.2 us (19%)
  between operations  13.3 us (3%)
  other arithmetic  12.8 us (3%)
  blocking collectives  6.33 us (1%)
    all_gather x1, waiting for transfers between devices, shards(): station_piece = lax.all_gather(jacobian, 'row', axis=0, tiled=True)  131 us
    all_gather x1, waiting for transfers between devices, shards(): lax.all_gather(row_part.astype(jnp.bfloat16), 'row', axis=0, tiled=True)  74.1 us
    dot_general x1, matrix products, shards(): jnp.einsum('ijra,jrb->iab', scaled, station_piece, preferred_element_type...  47.4 us
    unnamed x14, local copies, waits for them, and re-layouts  43.6 us
    select_n x1, local copies, waits for them, and re-layouts, shards(): jnp.where((piece_ids == panel_id)[None, None, :, None], panel_factor[:, :...  31.2 us
    dot_general x1, matrix products, shards(): jnp.einsum('iac,jcb->iajb', panel_factor, station_piece, precision=HIGHES...  28.2 us
    dot_general x1, matrix products, shards(): jnp.einsum('ijra,irb->iajb', scaled_all, slab_jac, preferred_element_type...  23.7 us
    psum x2, waiting for transfers between devices, broadcast(): return lax.psum(jnp.where(mine, value, jnp.zeros_like(value)), axis)  19.6 us
  transfers between devices with their start and end apart: 4, of which 3 were waited for; matrix products, arithmetic and copies ran while one was open for 15% of the time, Pallas kernels for 0%

profile of v1, /device:TPU:0, one launch (start us, length us, event | category | flops | bytes accessed | tf_op | source)
XLA Modules:
  0.0 444.3 jit_solution(7773262017936105153)
XLA Ops:
  6.5 0.7 all-gather.4.cloned.1.call-update
  7.3 1.0 convert_element_type.35
  8.5 130.7 %all-gather.4.cloned.1.call-done = bf16[256,256,128]{2,1,0:T(8,128)(2,1)} async-done(((bf16[16,256,128]{2,1,0:T(8,128)(2,1)}), bf16[256,256,128]{2,1,0:T(8,128)(2,1)}) %all-gather.4.cloned.1.call-update) | async-done | bytes 16777232 | tf_op jit(solution)/shard_map/all_gather | solution.py:26
  139.1 0.9 constant_dynamic-slice_fusion
  140.1 0.1 copy.49
  140.2 0.7 broadcast_select_fusion
  140.9 9.5 %convert_element_type.36 = f32[256,256,128]{2,1,0:T(8,128)S(1)} convert(bf16[256,256,128]{2,1,0:T(8,128)(2,1)} %all-gather.4.cloned.1.call-done) | non-fusion elementwise | flops 8388608 | bytes 50331648 | tf_op jit(solution)/shard_map/convert_element_type | solution.py:30
  150.4 47.4 %fusion.12 = f32[2,128,128]{2,1,0:T(8,128)S(1)} fusion(bf16[256,256,128]{2,1,0:T(8,128)(2,1)} %all-gather.4.cloned.1.call-done, f32[256,256,128]{2,1,0:T(8,128)S(1)} %convert_element_type.36, f32[2,256,256]{2,1,0:T(8,128)S(1)} %convert_element_type.35, pred[2,256]{1,0:T(4,128)(4,1)S(1)} %broadcast_compare_fusion), kind=kOutput, calls=%fused_computation.19 | convolution fusion | flops 4345298944 | bytes 50987520 | tf_op jit(solution)/shard_map/ijra,jrb->iab/dot_general | solution.py:32
  197.8 6.3 %all-gather = f32[4,128,128]{2,1,0:T(8,128)S(1)} all-gather(f32[2,128,128]{2,1,0:T(8,128)S(1)} %fusion.12), channel_id=2, replica_groups=mesh['row'=16,'col'=2] {'col'}, dimensions={0}, use_global_device_ids=true | all-gather | bytes 393216 | tf_op jit(solution)/shard_map/all_gather | solution.py:45
  204.2 4.6 %copy.33 = f32[2,128,128]{0,2,1:T(8,128)} copy(f32[2,128,128]{2,1,0:T(8,128)S(1)} %reduce_sum.9) | data formatting | bytes 262144 | tf_op jit(solution)/shard_map/reduce_sum | solution.py:45
  208.8 1.8 gather_fusion
  210.7 0.1 copy.35
  210.8 1.5 fusion.20
  212.2 23.7 %bitcast_select_fusion = f32[2,128,256,128]{1,3,2,0:T(8,128)S(1)} fusion(f32[2,128,128]{1,2,0:T(8,128)S(1)} %copy.35, pred[2,256]{1,0:T(4,128)(4,1)S(1)} %broadcast_compare_fusion, f32[256,256,128]{2,1,0:T(8,128)} %copy-done.1, f32[2,256,256]{2,1,0:T(8,128)S(1)} %convert_element_type.35, bf16[2,256,128]{1,2,0:T(8,128)(2,1)} %all-reduce.4.cloned.1.call-done), kind=kOutput, calls=%fused_computation.5 | convolution fusion | flops 4353687552 | bytes 67895808 | tf_op jit(solution)/shard_map/ijra,irb->iajb/dot_general | solution.py:42
  236.0 11.7 %copy-done.2 = f32[2,128,256,128]{1,3,2,0:T(8,128)} copy-done((f32[2,128,256,128]{1,3,2,0:T(8,128)}, f32[2,128,256,128]{1,3,2,0:T(8,128)S(1)}, u32[]{:S(2)}) %copy-start.2) | copy-done | bytes 33554456
  247.6 1.0 fusion.15
  248.7 0.2 all-gather.6.cloned.1.call-start
  248.9 19.6 %all-reduce.6.cloned.1.call-done = (bf16[2,128,128]{2,1,0:T(8,128)(2,1)}, bf16[256,128]{1,0:T(8,128)(2,1)}) async-done(((bf16[2,128,128]{2,1,0:T(8,128)(2,1)}, bf16[256,128]{1,0:T(8,128)(2,1)}), (bf16[2,128,128]{2,1,0:T(8,128)(2,1)}, bf16[256,128]{1,0:T(8,128)(2,1)})) %all-reduce.6.cloned.1.call-update) | async-done | bytes 131088 | tf_op jit(solution)/shard_map/psum | solution.py:11
  268.6 2.9 convolution_convert_fusion
  271.5 0.9 copy.38
  272.5 74.1 %all-gather.6.cloned.1.call-done = bf16[256,128,128]{2,1,0:T(8,128)(2,1)} async-done(((bf16[16,128,128]{2,1,0:T(8,128)(2,1)}), bf16[256,128,128]{2,1,0:T(8,128)(2,1)}) %all-gather.6.cloned.1.call-update) | async-done | bytes 8388624 | tf_op jit(solution)/shard_map/all_gather | solution.py:71
  346.6 28.2 %subtract_select_fusion = f32[2,128,256,128]{1,3,2,0:T(8,128)} fusion(f32[2,128,256,128]{1,3,2,0:T(8,128)} %copy-done.2, f32[2,128,128]{1,2,0:T(8,128)S(1)} %copy.38, pred[256]{0:T(512)(128)(4,1)S(1)} %broadcast_compare_fusion.1, bf16[256,128,128]{2,1,0:T(8,128)(2,1)} %all-gather.6.cloned.1.call-done, bf16[2,128,128]{2,1,0:T(8,128)(2,1)} %get-tuple-element.5), kind=kOutput, calls=%fused_computation.6 | convolution fusion | flops 2164260864 | bytes 75694336 | tf_op jit(solution)/shard_map/iac,jcb->iajb/dot_general | solution.py:76
  374.8 31.2 %copy.41 = f32[2,128,256,128]{3,2,1,0:T(8,128)} copy(f32[2,128,256,128]{1,3,2,0:T(8,128)} %subtract_select_fusion) | data formatting | bytes 67108864 | tf_op jit(solution)/shard_map/jit(_where)/select_n | solution.py:84
  406.0 31.8 %copy.52 = f32[32,8,256,128]{3,1,2,0:T(8,128)} copy(f32[32,8,256,128]{3,2,1,0:T(8,128)} %bitcast.48) | data formatting | bytes 67108864
  (30 shorter events, 0.4 us)
Async XLA Ops:
  6.5 241.1 %copy-start = (f32[128,128]{1,0:T(8,128)S(1)}, f32[128,128]{1,0:T(8,128)}, u32[]{:S(2)}) copy-start(f32[128,128]{1,0:T(8,128)} %param.9) | copy-start | bytes 196612
  6.5 132.6 %all-gather.4.cloned.1.call-start = ((), (), s32[]{:S(2)}) async-start(), calls=%async_computation | async-start | bytes 17825792 | tf_op jit(solution)/shard_map/all_gather | solution.py:26
  7.3 205.0 %all-reduce.4.cloned.1.call-start = ((), (), s32[]{:S(2)}) async-start(), calls=%async_computation.1 | async-start | bytes 262144 | tf_op jit(solution)/shard_map/psum | solution.py:11
  140.9 127.7 %all-reduce.6.cloned.1.call-start = ((), (), s32[]{:S(2)}) async-start(), calls=%async_computation.3 | async-start | bytes 262144 | tf_op jit(solution)/shard_map/psum | solution.py:11
  150.4 47.4 %copy-start.1 = (f32[256,256,128]{2,1,0:T(8,128)}, f32[256,256,128]{2,1,0:T(8,128)S(1)}, u32[]{:S(2)}) copy-start(f32[256,256,128]{2,1,0:T(8,128)S(1)} %convert_element_type.36) | copy-start | bytes 100663296
  150.4 60.2 %copy-start.5 = (f32[2,128]{1,0:T(2,128)S(1)}, f32[2,128]{1,0:T(2,128)}, u32[]{:S(2)}) copy-start(f32[2,128]{1,0:T(2,128)} %param.8) | copy-start | bytes 3076
  212.2 36.7 %copy-start.4 = (bf16[16,256]{1,0:T(8,128)(2,1)S(1)}, bf16[16,256]{1,0:T(8,128)(2,1)}, u32[]{:S(2)}) copy-start(bf16[16,256]{1,0:T(8,128)(2,1)} %param.7) | copy-start | bytes 24580
  212.2 56.4 %copy-start.3 = (bf16[16,256,128]{2,1,0:T(8,128)(2,1)S(1)}, bf16[16,256,128]{2,1,0:T(8,128)(2,1)}, u32[]{:S(2)}) copy-start(bf16[16,256,128]{2,1,0:T(8,128)(2,1)} %param.5) | copy-start | bytes 3145732
  236.0 11.7 %copy-start.2 = (f32[2,128,256,128]{1,3,2,0:T(8,128)}, f32[2,128,256,128]{1,3,2,0:T(8,128)S(1)}, u32[]{:S(2)}) copy-start(f32[2,128,256,128]{1,3,2,0:T(8,128)S(1)} %bitcast_select_fusion) | copy-start | bytes 100663296
  248.7 97.9 %all-gather.6.cloned.1.call-start = ((), (), s32[]{:S(2)}) async-start(), calls=%async_computation.2 | async-start | bytes 8912896 | tf_op jit(solution)/shard_map/all_gather | solution.py:71
Sparse Core Ops, SparseCore 0:
  9.5 129.5 all-gather.3
  141.4 19.5 all-reduce.3
  248.8 19.7 all-reduce.5
  271.6 74.8 all-gather.5
